TPU v7x, 128 devices: a whole 4x4x4 slice. The times are simulated.
128 devices in a mesh: ctx: 8 (over y, x_hi), head: 16 (over x_lo, z, core).
Axes of the slice: x: 4 (x_hi: 2, x_lo: 2; x = x_hi * 2 + x_lo), y: 4, z: 4, core: 2. Of those that a mesh axis runs over, the one named last changes fastest.
Arguments:
- queries: bfloat16 [2, 4096, 4096], P(None, 'ctx', 'head'), may hold values from -6 to 6
- keys: bfloat16 [2, 4096, 4096], P(None, 'ctx', 'head'), may hold values from -6 to 6
- values: bfloat16 [2, 4096, 4096], P(None, 'ctx', 'head'), may hold values from -6 to 6
- rates: float32 [16, 2, 4096], P('head', None, 'ctx'), may hold values from 0.05 to 1
- w_gate: float32 [16, 256, 512], P('head'), may hold values from -0.375 to 0.375
- w_up: float32 [16, 256, 512], P('head'), may hold values from -0.375 to 0.375
- w_down: float32 [16, 512, 256], P('head'), may hold values from -0.25 to 0.25
- gains: float32 [16, 256], P('head'), may hold values from 0.25 to 0.6
- out_proj: bfloat16 [4096, 4096], P('head'), may hold values from -0.125 to 0.125
Outputs:
- output: bfloat16 [2, 4096, 4096], P(None, 'ctx', 'head')
All inputs are finite; a program needn't handle non-finite values.
Results may differ from a plain program's by a relative error of at most 0.0051.
Values may be sent and summed in bfloat16 or wider, within the bound.
A program may use at most 128 MiB of HBM per device.

v0:
```python
import jax
import jax.numpy as jnp
from jax import lax
from jax.sharding import PartitionSpec as P

WINDOW = 256
NS_ITERS = 5


highest = lax.Precision.HIGHEST
attn_temp = 5.0
step_size = 0.5
quintic_one = 3.4445
quintic_two = -4.775
quintic_three = 2.0315


def passed_along(value, axis, steps):
    count = lax.axis_size(axis)
    pairs = [(source, (source + steps) % count) for source in range(count)]
    return lax.ppermute(value, axis, pairs)


def unit_rows(matrix):
    return matrix / jnp.sqrt(jnp.sum(matrix * matrix, axis=-1, keepdims=True) + 1e-06)


def exact_dot(left, right):
    return jnp.dot(left, right, precision=highest, preferred_element_type=jnp.float32)


def fast_grads(key_unit, value_rows, rate_rows, w_gate, w_up, w_down):
    gate_pre = exact_dot(key_unit, w_gate)
    up_pre = exact_dot(key_unit, w_up)
    sigma = jax.nn.sigmoid(gate_pre)
    gate_act = gate_pre * sigma
    hidden = gate_act * up_pre
    target = rate_rows[:, None] * value_rows
    grad_down = exact_dot(hidden.T, target)
    back_hidden = exact_dot(target, w_down.T)
    slope = sigma * (1.0 + gate_pre * (1.0 - sigma))
    grad_gate = exact_dot(key_unit.T, back_hidden * up_pre * slope)
    grad_up = exact_dot(key_unit.T, back_hidden * gate_act)
    return jnp.stack([grad_gate, grad_up, grad_down.T])


def quintic_step(gram, iterate):
    poly = quintic_two * gram + quintic_three * jnp.einsum(
        "mij,mjk->mik", gram, gram, precision=highest
    )
    return quintic_one * iterate + jnp.einsum("mij,mjk->mik", poly, iterate, precision=highest)


def orthogonal(grads):
    norms = jnp.sqrt(jnp.sum(grads * grads, axis=(1, 2), keepdims=True)) + 1e-06
    iterate = grads / norms
    for sweep_at in range(NS_ITERS):
        gram = jnp.einsum("mik,mjk->mij", iterate, iterate, precision=highest)
        iterate = quintic_step(gram, iterate)
    return iterate


def apply_fast(query_unit, w_gate, w_up, w_down):
    gate_pre = exact_dot(query_unit, w_gate)
    gate_act = gate_pre * jax.nn.sigmoid(gate_pre)
    return exact_dot(gate_act * exact_dot(query_unit, w_up), w_down)


def band_attention(query_half, ext_keys, ext_values, masked_head):
    local_rows = query_half.shape[0]
    block_rows = min(512, local_rows)
    scores = lax.dot_general(
        query_half, ext_keys, (((1,), (1,)), ((), ())), preferred_element_type=jnp.float32
    )
    query_pos = jnp.arange(block_rows, dtype=jnp.int32)[:, None]
    key_pos = jnp.arange(block_rows + WINDOW, dtype=jnp.int32)[None, :]
    distance = query_pos + WINDOW - key_pos
    valid = (distance >= 0) & (distance < WINDOW)
    if masked_head is not None:
        valid = valid & ((key_pos + 0 >= WINDOW) | jnp.logical_not(masked_head))
    weights = jnp.where(valid, jnp.exp(attn_temp * (scores - 1.0)), 0.0)
    probs = (weights / jnp.sum(weights, axis=-1, keepdims=True)).astype(jnp.bfloat16)
    outputs = jnp.dot(probs, ext_values, preferred_element_type=jnp.float32)
    return outputs


def body(queries, keys, values, rates, w_gate, w_up, w_down, gains, out_proj):
    group_count, local_rows, head_width = queries.shape
    first_device = lax.axis_index("ctx") == 0
    query_unit = unit_rows(queries.astype(jnp.float32))
    key_unit = unit_rows(keys.astype(jnp.float32))
    query_half = query_unit.astype(jnp.bfloat16)
    key_half = key_unit.astype(jnp.bfloat16)
    tails = jnp.stack([key_half[:, local_rows - WINDOW :], values[:, local_rows - WINDOW :]])
    prior = passed_along(tails, "ctx", 1)
    gate_now = w_gate[0]
    up_now = w_up[0]
    down_now = w_down[0]
    mixed = []
    for group_at in range(group_count):
        if group_at == 0:
            halo_rows = prior[:, 0]
            masked_head = first_device
        else:
            halo_rows = jnp.where(first_device, prior[:, group_at - 1], prior[:, group_at])
            masked_head = None
        ext_keys = jnp.concatenate([halo_rows[0], key_half[group_at]], axis=0)
        ext_values = jnp.concatenate([halo_rows[1], values[group_at]], axis=0)
        attended = band_attention(query_half[group_at], ext_keys, ext_values, masked_head)
        grads = fast_grads(
            key_unit[group_at],
            values[group_at].astype(jnp.float32),
            rates[0, group_at],
            gate_now,
            up_now,
            down_now,
        )
        ortho = orthogonal(lax.psum(grads, "ctx"))
        gate_now = gate_now + step_size * ortho[0]
        up_now = up_now + step_size * ortho[1]
        down_now = down_now + step_size * ortho[2].T
        fast_out = apply_fast(query_unit[group_at], gate_now, up_now, down_now)
        normed = (
            fast_out
            * lax.rsqrt(jnp.mean(fast_out * fast_out, axis=-1, keepdims=True) + 1e-05)
            * gains[0]
        )
        mixed.append((attended + normed).astype(jnp.bfloat16))
    combined = jnp.stack(mixed)
    proj_columns = lax.all_to_all(out_proj, "head", split_axis=1, concat_axis=0, tiled=True)
    summed = jnp.einsum(
        "ctf,fo->cto",
        lax.all_gather(combined, "head", axis=2, tiled=True),
        proj_columns,
        preferred_element_type=jnp.float32,
    )
    return summed.astype(jnp.bfloat16)


def solution(mesh):
    return jax.shard_map(
        body,
        mesh=mesh,
        in_specs=(
            P(None, "ctx", "head"),
            P(None, "ctx", "head"),
            P(None, "ctx", "head"),
            P("head", None, "ctx"),
            P("head", None, None),
            P("head", None, None),
            P("head", None, None),
            P("head", None),
            P("head", None),
        ),
        out_specs=P(None, "ctx", "head"),
        check_vma=False,
    )
```

profile of v0, /device:TPU:1, one launch (start us, length us, event | category | flops | bytes accessed | tf_op | source)
XLA Modules:
  0.0 371.3 jit_solution(8970687296122975035)
XLA Ops:
  6.5 1.3 fusion.18
  7.9 1.2 convert_divide_fusion
  10.1 3.6 collective-permute-start
  13.6 1.0 fusion.61
  14.7 1.0 fusion.63
  15.7 1.0 fusion.52
  16.8 1.3 convolution_bitcast_fusion.4
  18.1 1.4 convolution_bitcast_fusion.5
  19.5 1.4 convolution_bitcast_fusion.3
  20.9 1.3 pad_maximum_fusion
  23.2 1.3 fusion.17
  24.5 1.0 copy.10
  26.3 1.2 convert_divide_fusion.1
  28.0 1.1 slice_select_fusion
  29.7 1.6 slice_bitcast_fusion.28
  31.3 2.0 fusion.127
  33.4 82.2 %all-reduce.3.cloned.1.call-done = f32[3,256,512]{2,1,0:T(8,128)} async-done(((f32[3,256,512]{2,1,0:T(8,128)}), f32[3,256,512]{2,1,0:T(8,128)}) %all-reduce.3.cloned.1.call-update) | async-done | bytes 1572880 | tf_op jit(solution)/shard_map/psum | solution.py:118
  115.5 1.8 multiply_reduce_fusion.1
  117.4 1.8 fusion.85
  119.3 0.9 fusion.12
  120.2 1.8 multiply_add_fusion.9
  122.0 1.7 fusion.128
  123.7 0.9 fusion.11
  124.6 1.6 multiply_add_fusion.8
  126.2 2.1 fusion.129
  129.2 1.6 multiply_add_fusion.7
  130.8 1.7 fusion.130
  133.4 1.6 multiply_add_fusion.6
  135.0 1.7 fusion.131
  137.6 1.6 multiply_add_fusion.5
  139.2 1.0 fusion.57
  140.3 1.2 fusion.54
  141.5 1.1 fusion.66
  142.6 1.3 convolution_bitcast_fusion.1
  143.9 1.4 convolution_bitcast_fusion.2
  145.3 1.4 convolution_bitcast_fusion
  146.7 1.3 pad_maximum_fusion.1
  148.1 1.0 copy-done.17
  149.1 2.0 fusion.126
  151.1 1.0 fusion.59
  152.1 1.2 convolution_multiply_fusion.1
  153.3 1.9 multiply_reduce_fusion.3
  155.2 2.0 copy.11
  157.3 2.8 fusion.16
  160.0 83.2 %all-reduce.5.cloned.1.call-done = f32[3,256,512]{2,1,0:T(8,128)} async-done(((f32[3,256,512]{2,1,0:T(8,128)}), f32[3,256,512]{2,1,0:T(8,128)}) %all-reduce.5.cloned.1.call-update) | async-done | bytes 1572880 | tf_op jit(solution)/shard_map/psum | solution.py:118
  243.3 1.8 multiply_reduce_fusion
  245.2 1.8 fusion.86
  247.0 0.9 fusion.7
  247.9 1.8 multiply_add_fusion.4
  249.7 1.7 fusion.132
  252.4 2.0 multiply_add_fusion.3
  254.3 1.7 fusion.133
  257.0 1.6 multiply_add_fusion.2
  258.5 1.7 fusion.134
  261.1 1.6 multiply_add_fusion.1
  262.7 1.7 fusion.135
  265.3 1.8 multiply_add_fusion
  267.1 1.1 fusion.46
  268.2 1.2 convolution_multiply_fusion
  269.4 1.2 multiply_reduce_fusion.2
  270.8 2.0 fusion.15
  273.9 43.4 %all_to_all.19 = bf16[256,16,256]{2,0,1:T(8,128)(2,1)S(1)} all-to-all(bf16[256,16,256]{2,0,1:T(8,128)(2,1)S(1)} %bitcast.208), channel_id=1, replica_groups=mesh['ctx'=8,'head'=16] {'head'}, dimensions={1} | all-to-all | bytes 4194304 | tf_op jit(solution)/shard_map/all_to_all | solution.py:130
  317.4 40.8 %all-gather.2.cloned.1.call-done = bf16[2,512,4096]{2,1,0:T(8,128)(2,1)} async-done(((bf16[2,512,256]{2,1,0:T(8,128)(2,1)}), bf16[2,512,4096]{2,1,0:T(8,128)(2,1)}) %all-gather.2.cloned.1.call-update) | async-done | bytes 8388624 | tf_op jit(solution)/shard_map/all_gather | solution.py:133
  358.1 6.5 %convolution_convert_fusion = bf16[2,512,256]{2,1,0:T(8,128)(2,1)} fusion(bf16[2,512,4096]{2,1,0:T(8,128)(2,1)} %all-gather.2.cloned.1.call-done, bf16[4096,256,1]{1,0,2:T(8,128)(2,1)S(1)} %bitcast.210), kind=kOutput, calls=%fused_computation.29 | convolution fusion | flops 2147745792 | bytes 11010048 | tf_op jit(solution)/shard_map/ctf,fo->cto/dot_general | solution.py:131
  (76 shorter events, 12.1 us)
Async XLA Ops:
  6.5 2.6 copy-start.5
  6.5 109.0 %all-reduce.3.cloned.1.call-start = ((), (), s32[]{:S(2)}) async-start(), calls=%async_computation.1 | async-start | bytes 3145728 | tf_op jit(solution)/shard_map/psum | solution.py:118
  9.1 4.5 %copy-start.21 = (f32[1,2,512]{2,1,0:T(2,128)S(1)}, f32[1,2,512]{2,1,0:T(2,128)}, u32[]{:S(2)}) copy-start(f32[1,2,512]{2,1,0:T(2,128)} %param.12) | copy-start | bytes 12292
  9.1 4.5 %copy-start = (f32[1,256,512]{2,1,0:T(8,128)S(1)}, f32[1,256,512]{2,1,0:T(8,128)}, u32[]{:S(2)}) copy-start(f32[1,256,512]{2,1,0:T(8,128)} %param.13) | copy-start | bytes 1572868
  9.2 5.5 %copy-start.8 = (f32[1,256,512]{2,1,0:T(8,128)S(1)}, f32[1,256,512]{2,1,0:T(8,128)}, u32[]{:S(2)}) copy-start(f32[1,256,512]{2,1,0:T(8,128)} %param.14) | copy-start | bytes 1572868
  10.1 17.9 %collective-permute-start = (bf16[2,2,256,256]{3,2,1,0:T(8,128)(2,1)}, bf16[2,2,256,256]{3,2,1,0:T(8,128)(2,1)}, u32[]{:S(2)}, u32[]{:S(2)}) collective-permute-start(bf16[2,2,256,256]{3,2,1,0:T(8,128)(2,1)} %pad_maximum_fusion.2), channel_id=1, source_target_pairs={{0,16},{16,32},{32,48},{48,64},{64,80},{80,96},{96,112},{112,0},{1... | collective-permute-start | bytes 1572872 | tf_op jit(solution)/shard_map/ppermute | solution.py:21
  14.7 1.0 copy-start.11
  22.1 2.4 copy-start.12
  22.2 221.1 %all-reduce.5.cloned.1.call-start = ((), (), s32[]{:S(2)}) async-start(), calls=%async_computation.2 | async-start | bytes 3145728 | tf_op jit(solution)/shard_map/psum | solution.py:118
  23.2 3.1 copy-start.13
  27.5 5.9 %copy-start.16 = (bf16[2,512,256]{2,1,0:T(8,128)(2,1)}, bf16[2,512,256]{2,1,0:T(8,128)(2,1)S(1)}, u32[]{:S(2)}) copy-start(bf16[2,512,256]{2,1,0:T(8,128)(2,1)S(1)} %get-tuple-element.6) | copy-start | bytes 1572868
  115.5 1.9 copy-start.14
  139.2 1.1 copy-start.9
  140.2 1.3 copy-start.1
  140.3 1.3 copy-start.6
  148.0 1.0 copy-start.17
  148.0 1.1 copy-start.18
  148.0 1.1 copy-start.20
  148.0 210.1 %all-gather.2.cloned.1.call-start = ((), (), s32[]{:S(2)}) async-start(), calls=%async_computation.3 | async-start | bytes 8912896 | tf_op jit(solution)/shard_map/all_gather | solution.py:133
  149.1 2.0 copy-start.3
  151.1 1.1 copy-start.10
  152.1 1.2 copy-start.2
  153.3 3.9 %copy-start.22 = (f32[1,256]{1,0:T(1,128)S(1)}, f32[1,256]{1,0:T(1,128)}, u32[]{:S(2)}) copy-start(f32[1,256]{1,0:T(1,128)} %param.16) | copy-start | bytes 3076
  243.3 1.9 copy-start.15
  265.3 1.8 copy-start.4
  270.8 2.0 copy-start.19
  270.8 2.9 copy-start.7
Sparse Core Ops, SparseCore 0:
  22.3 93.2 all-reduce.2
  148.1 95.1 all-reduce.4
  273.8 84.2 all-gather.1
where the time goes:
time: 378 us; the launch traced here: 371 us
  waiting for transfers between devices  207 us (55%)
  matrix products  80.8 us (21%)
  blocking collectives  43.4 us (11%)
  other arithmetic  14 us (4%)
  between operations  13.9 us (4%)
  local copies, waits for them, and re-layouts  8.64 us (2%)
  starting transfers between devices  3.82 us (1%)
    psum x2, waiting for transfers between devices, body(): ortho = orthogonal(lax.psum(grads, 'ctx'))  165 us
    all_to_all x1, blocking collectives, body(): lax.all_to_all(out_proj, 'head', split_axis=1, concat_axis=0, tiled=True)  43.4 us
    all_gather x1, waiting for transfers between devices, body(): lax.all_gather(combined, 'head', axis=2, tiled=True)  40.8 us
    dot_general x18, matrix products, exact_dot(): jnp.dot(left, right, precision=highest, preferred_element_type=jnp.float32)  22.1 us
    dot_general x10, matrix products, orthogonal(): gram = jnp.einsum('mik,mjk->mij', iterate, iterate, precision=highest)  17.3 us
    dot_general x10, matrix products, quintic_step(): jnp.einsum('mij,mjk->mik', poly, iterate, precision=highest)  16.8 us
    dot_general x10, matrix products, quintic_step(): jnp.einsum('mij,mjk->mik', gram, gram, precision=highest)  9.34 us
  transfers between devices with their start and end apart: 4, of which 4 were waited for; matrix products, arithmetic and copies ran while one was open for 8% of the time, Pallas kernels for 0%

commit v1 on v0

v1 whole, which is shorter than its diff:
```python
import functools
import jax
import jax.numpy as jnp
from jax import lax
from jax.experimental import pallas as pl
from jax.experimental.pallas import tpu as pltpu
from jax.sharding import PartitionSpec as P

WINDOW = 256
NS_ITERS = 5
MESH = pl.DeviceIdType.MESH
bf16 = jnp.bfloat16
f32 = jnp.float32

NN = (((1,), (0,)), ((), ()))
NT = (((1,), (1,)), ((), ()))
COPIES = 120


def split(x):
    high = x.astype(bf16)
    return high, (x - high.astype(f32)).astype(bf16)


def dot1(a, b, dims=NN):
    return lax.dot_general(a, b, dims, preferred_element_type=f32)


def dot3(a, b, dims=NN):
    return dot1(a[0], b[0], dims) + (dot1(a[0], b[1], dims) + dot1(a[1], b[0], dims))


def unit_rows(x):
    return x / jnp.sqrt(jnp.sum(x * x, axis=-1, keepdims=True) + 1e-06)


def kernel(
    q_ref, k_ref, v_ref, rate_ref, gate_ref, up_ref, downt_ref, gain_ref, proj_ref,
    out_ref,
    gate_now, up_now, down_now, sums, part, yslot, xown, xslot, full, halo, attended, projg, gath, iterate,
    send_sem, recv_sem, local_sem,
):
    ctx = lax.axis_index("ctx")
    head = lax.axis_index("head")
    yi, xh = ctx // 2, ctx % 2
    xl, z, core = head // 8, (head // 2) % 4, head % 2
    first = ctx == 0

    barrier = pltpu.get_barrier_semaphore()
    for d in range(1, 8):
        pl.semaphore_signal(barrier, inc=1, device_id={"ctx": lax.rem(ctx + d, 8)}, device_id_type=MESH)
    for d in range(1, 16):
        pl.semaphore_signal(barrier, inc=1, device_id={"head": lax.rem(head + d, 16)}, device_id_type=MESH)

    started = []

    def send(src, dst, where):
        at = len(started)
        copy = pltpu.make_async_remote_copy(
            src_ref=src, dst_ref=dst, send_sem=send_sem.at[at], recv_sem=recv_sem.at[at],
            device_id=where, device_id_type=MESH,
        )
        copy.start()
        started.append(copy)
        return copy

    def rows64(index):
        return pl.ds(pl.multiple_of(index * 64, 64), 64)

    def halo_send(group):
        there = {"ctx": lax.rem(ctx + 1, 8)}
        return [
            send(ref.at[group, pl.ds(256, 256)], halo.at[group, at], there)
            for at, ref in enumerate((k_ref, v_ref))
        ]

    gate_now[...] = gate_ref[0]
    up_now[...] = up_ref[0]
    down_now[...] = downt_ref[0]

    def reduce_start(group, which, value):
        part[group, which] = value.astype(bf16)
        own = []
        for d in (2, 1, 3):
            there = lax.rem(yi + d, 4)
            own.append(
                send(
                    part.at[group, which, rows64(there)],
                    yslot.at[group, which, d - 1],
                    {"ctx": there * 2 + xh},
                )
            )
        return own

    def fast_grads(group, ready=None):
        key_unit = unit_rows(k_ref[group].astype(f32))
        key_two = split(key_unit)
        key_t = split(key_unit.T)
        gate_pre = dot3(key_two, split(gate_now[...]))
        up_pre = dot3(key_two, split(up_now[...]))
        target = rate_ref[group] * v_ref[group].astype(f32)
        sigma = jax.nn.sigmoid(gate_pre)
        gate_act = gate_pre * sigma
        grad_down = dot3(split(target.T), split(gate_act * up_pre))
        if ready is not None:
            ready()
        sends = {2: reduce_start(group, 2, grad_down)}
        back = dot3(split(target), split(down_now[...]))
        sends[1] = reduce_start(group, 1, dot3(key_t, split(back * gate_act)))
        slope = sigma * (1.0 + gate_pre * (1.0 - sigma))
        sends[0] = reduce_start(group, 0, dot3(key_t, split(back * up_pre * slope)))
        return sends

    def reduce_second(group, which, sends):
        for copy in sends:
            copy.wait_recv()
        total = part[group, which, rows64(yi)].astype(f32)
        for slot in range(3):
            total = total + yslot[group, which, slot].astype(f32)
        xown[group, which] = total.astype(bf16)
        return send(xown.at[group, which], xslot.at[group, which], {"ctx": yi * 2 + (1 - xh)})

    def reduce_third(group, which, copy):
        copy.wait_recv()
        total = xown[group, which].astype(f32) + xslot[group, which].astype(f32)
        full[group, which, rows64(yi)] = total.astype(bf16)
        return [
            send(
                full.at[group, which, rows64(yi)],
                full.at[group, which, rows64(yi)],
                {"ctx": lax.rem(yi + d, 4) * 2 + xh},
            )
            for d in (2, 1, 3)
        ]

    def orthogonal(group, which, now):
        grads = full[group, which].astype(f32)
        norm = jnp.sqrt(jnp.sum(grads * grads, keepdims=True)) + 1e-06
        iterate[...] = grads / norm

        def sweep(_, carry):
            x = iterate[...]
            x2 = split(x)
            gram = dot3(x2, x2, NT)
            g2 = split(gram)
            poly = -4.775 * gram + 2.0315 * dot3(g2, g2)
            iterate[...] = 3.4445 * x + dot3(split(poly), x2)
            return carry

        lax.fori_loop(0, NS_ITERS, sweep, 0)
        now[...] = now[...] + 0.5 * iterate[...]

    def attend(group):
        if group == 0:
            prior = 0
        else:
            prior = jnp.where(first, 0, 1)
        query = unit_rows(q_ref[group].astype(f32)).astype(bf16)
        key = unit_rows(k_ref[group].astype(f32)).astype(bf16)
        halo_key = unit_rows(halo[prior, 0].astype(f32)).astype(bf16)
        query_pos = lax.broadcasted_iota(jnp.int32, (256, 512), 0)
        key_pos = lax.broadcasted_iota(jnp.int32, (256, 512), 1)
        distance = query_pos + WINDOW - key_pos
        band = (distance >= 0) & (distance < WINDOW)
        for block in range(2):
            if block == 0:
                keys = jnp.concatenate([halo_key, key[:256]], axis=0)
                vals = jnp.concatenate([halo[prior, 1], v_ref[group, 0:256]], axis=0)
            else:
                keys = key
                vals = v_ref[group]
            scores = dot1(query[block * 256 : block * 256 + 256], keys, NT)
            valid = band
            if block == 0 and group == 0:
                valid = band & (key_pos >= jnp.where(first, WINDOW, 0))
            weights = jnp.where(valid, jnp.exp(5.0 * (scores - 1.0)), 0.0)
            probs = (weights / jnp.sum(weights, axis=-1, keepdims=True)).astype(bf16)
            attended[group, block * 256 : block * 256 + 256] = dot1(probs, vals)

    def apply_fast(group):
        query = split(unit_rows(q_ref[group].astype(f32)))
        gate_pre = dot3(query, split(gate_now[...]))
        hidden = gate_pre * jax.nn.sigmoid(gate_pre) * dot3(query, split(up_now[...]))
        fast = dot3(split(hidden), split(down_now[...]), NT)
        normed = fast * lax.rsqrt(jnp.mean(fast * fast, axis=-1, keepdims=True) + 1e-05) * gain_ref[...]
        gath[group, head] = (attended[group] + normed).astype(bf16)

    def name(xl_at, z_at, core_at):
        return xl_at * 8 + lax.rem(z_at + 4, 4) * 2 + core_at

    sibling = {"head": name(xl, z, 1 - core)}
    above = {"head": name(xl, z + 1, core)}
    below = {"head": name(xl, z - 1, core)}
    across = {"head": name(1 - xl, z, core)}

    def block_send(group, owner, where, rows=None):
        ref = gath.at[group, owner] if rows is None else gath.at[group, owner, rows]
        return send(ref, ref, where)

    def gather_one(group):
        return {
            "sib": block_send(group, head, sibling),
            "x": block_send(group, head, across),
            "zp": block_send(group, head, above),
            "zm": block_send(group, head, below),
        }

    def gather_two(group, c):
        c["zp"].wait_recv()
        c["f1"] = block_send(group, name(xl, z - 1, core), above, pl.ds(0, 256))
        c["s1"] = block_send(group, name(xl, z - 1, core), sibling)
        c["zm"].wait_recv()
        c["f2"] = block_send(group, name(xl, z + 1, core), below, pl.ds(256, 256))
        c["s2"] = block_send(group, name(xl, z + 1, core), sibling)
        c["x"].wait_recv()
        c["xp"] = block_send(group, name(1 - xl, z, core), above)
        c["xm"] = block_send(group, name(1 - xl, z, core), below)
        c["s3"] = block_send(group, name(1 - xl, z, core), sibling)

    def gather_three(group, c):
        c["f1"].wait_recv()
        c["f2"].wait_recv()
        c["x2"] = block_send(group, name(xl, z + 2, core), across)
        c["s4"] = block_send(group, name(xl, z + 2, core), sibling)
        c["xp"].wait_recv()
        c["s5"] = block_send(group, name(1 - xl, z - 1, core), sibling)
        c["xm"].wait_recv()
        c["s6"] = block_send(group, name(1 - xl, z + 1, core), sibling)

    def gather_four(group, c):
        c["x2"].wait_recv()
        c["s7"] = block_send(group, name(1 - xl, z + 2, core), sibling)

    def arrived(c):
        for key in ("sib", "s1", "s2", "s3", "s4", "s5", "s6", "s7"):
            c[key].wait_recv()

    def project(group):
        total = None
        for at in range(16):
            term = dot1(gath[group, at], projg[at])
            total = term if total is None else total + term
        out_ref[group] = total.astype(bf16)

    halos = []

    def on_ready():
        pl.semaphore_wait(barrier, 22)

    def on_ready_one():
        return

    sends = fast_grads(0, on_ready)
    halos.append(halo_send(0))
    cross = {which: reduce_second(0, which, sends[which]) for which in (2, 1, 0)}
    spread = {which: reduce_third(0, which, cross[which]) for which in (2, 1, 0)}
    halos.append(halo_send(1))
    mine = pltpu.make_async_copy(
        proj_ref.at[:, pl.ds(pl.multiple_of(head * 256, 256), 256)], projg.at[head], local_sem
    )
    mine.start()
    exchange = []
    for d in range(1, 16):
        there = lax.rem(head + d, 16)
        exchange.append(
            send(
                proj_ref.at[:, pl.ds(pl.multiple_of(there * 256, 256), 256)],
                projg.at[head],
                {"head": there},
            )
        )
    for copy in halos[0]:
        copy.wait_recv()
    attend(0)
    for which, now in ((2, down_now), (1, up_now), (0, gate_now)):
        for copy in spread[which]:
            copy.wait_recv()
        orthogonal(0, which, now)

    sends = fast_grads(1)
    apply_fast(0)
    near = gather_one(0)
    cross = {which: reduce_second(1, which, sends[which]) for which in (2, 1, 0)}
    for copy in halos[1]:
        copy.wait_recv()
    spread = {which: reduce_third(1, which, cross[which]) for which in (2, 1, 0)}
    attend(1)
    gather_two(0, near)
    for which, now in ((2, down_now), (1, up_now), (0, gate_now)):
        for copy in spread[which]:
            copy.wait_recv()
        orthogonal(1, which, now)
        if which == 2:
            gather_three(0, near)
        if which == 1:
            gather_four(0, near)
    apply_fast(1)
    last = gather_one(1)
    mine.wait()
    for copy in exchange:
        copy.wait_recv()
    arrived(near)
    project(0)
    gather_two(1, last)
    gather_three(1, last)
    gather_four(1, last)
    arrived(last)
    project(1)
    for copy in started:
        copy.wait_send()


def body(queries, keys, values, rates, w_gate, w_up, w_down, gains, out_proj):
    groups, rows, width = queries.shape
    hidden = w_gate.shape[2]
    vmem = pl.BlockSpec(memory_space=pltpu.VMEM)
    return pl.pallas_call(
        kernel,
        out_shape=jax.ShapeDtypeStruct((groups, rows, width), bf16),
        in_specs=[vmem] * 8 + [pl.BlockSpec(memory_space=pl.ANY)],
        out_specs=vmem,
        scratch_shapes=[
            pltpu.VMEM((width, hidden), f32),
            pltpu.VMEM((width, hidden), f32),
            pltpu.VMEM((width, hidden), f32),
            pltpu.VMEM((8, 128), f32),
            pltpu.VMEM((2, 3, width, hidden), bf16),
            pltpu.VMEM((2, 3, 3, 64, hidden), bf16),
            pltpu.VMEM((2, 3, 64, hidden), bf16),
            pltpu.VMEM((2, 3, 64, hidden), bf16),
            pltpu.VMEM((2, 3, width, hidden), bf16),
            pltpu.VMEM((2, 2, WINDOW, width), bf16),
            pltpu.VMEM((2, rows, width), f32),
            pltpu.VMEM((16, width, width), bf16),
            pltpu.VMEM((2, 16, rows, width), bf16),
            pltpu.VMEM((width, hidden), f32),
            pltpu.SemaphoreType.DMA((COPIES,)),
            pltpu.SemaphoreType.DMA((COPIES,)),
            pltpu.SemaphoreType.DMA,
        ],
        compiler_params=pltpu.CompilerParams(
            collective_id=0, has_side_effects=True, vmem_limit_bytes=62 * 1024 * 1024
        ),
    )(
        queries, keys, values, rates[0][:, :, None], w_gate, w_up, jnp.swapaxes(w_down, 1, 2), gains, out_proj
    )


def solution(mesh):
    return jax.shard_map(
        body,
        mesh=mesh,
        in_specs=(
            P(None, "ctx", "head"),
            P(None, "ctx", "head"),
            P(None, "ctx", "head"),
            P("head", None, "ctx"),
            P("head", None, None),
            P("head", None, None),
            P("head", None, None),
            P("head", None),
            P("head", None),
        ),
        out_specs=P(None, "ctx", "head"),
        check_vma=False,
    )
```

time: 378 us -> 131 us (0.35); the launches traced: 371 us -> 130 us
  waiting for transfers between devices: 207 us -> 0 us
  Pallas kernels: 0 us -> 124 us
  matrix products: 80.8 us -> 0 us
  blocking collectives: 43.4 us -> 0 us
  other arithmetic: 14 us -> 0 us
  between operations: 13.9 us -> 0.01 us
  starting transfers between devices: 3.82 us -> 0 us
    psum x2 -> x0, waiting for transfers between devices: 165 us -> none  [body(): ortho = orthogonal(lax.psum(grads, 'ctx'))]
    pallas_call x0 -> x1, Pallas kernels: none -> 124 us  [body(): pl.pallas_call(kernel, out_shape=jax.ShapeDtypeStruct((groups, rows, widt...]
    dot_general x53 -> x0, matrix products: 80.8 us -> none  [the longest x18 22.1 us: exact_dot(): jnp.dot(left, right, precision=highest, preferred_element_type=jnp.float32)]
    all_to_all x1 -> x0, blocking collectives: 43.4 us -> none  [body(): lax.all_to_all(out_proj, 'head', split_axis=1, concat_axis=0, tiled=True)]
    all_gather x1 -> x0, waiting for transfers between devices: 40.8 us -> none  [body(): lax.all_gather(combined, 'head', axis=2, tiled=True)]
    reduce_sum x4 -> x0, other arithmetic: 6.2 us -> none  [the longest x2 3.56 us: orthogonal(): norms = jnp.sqrt(jnp.sum(grads * grads, axis=(1, 2), keepdims=True)) + 1e-06]
    another operation x4 -> x0, other arithmetic: 4.22 us -> none  [the longest x2 2.54 us: fast_grads(): return jnp.stack([grad_gate, grad_up, grad_down.T])]
    squeeze x4 -> x0, local copies, waits for them, and re-layouts: 3.82 us -> none  [the longest x3 3.06 us: body(): ext_values = jnp.concatenate([halo_rows[1], values[group_at]], axis=0)]
  transfers between devices with their start and end apart: 4 -> 0, of which waited for: 4 -> 0; matrix products, arithmetic and copies ran while one was open for 8% -> 0% of each run, Pallas kernels for 0% -> 0%
where the time goes in v1:
time: 131 us; the launch traced here: 130 us
  Pallas kernels  124 us (95%)
  local copies, waits for them, and re-layouts  5.61 us (4%)
    pallas_call x1, Pallas kernels, body(): pl.pallas_call(kernel, out_shape=jax.ShapeDtypeStruct((groups, rows, widt...  124 us
    unnamed x2, local copies, waits for them, and re-layouts  3.9 us

profile of v1, /device:TPU:1, one launch (start us, length us, event | category | flops | bytes accessed | tf_op | source)
XLA Modules:
  0.0 129.5 jit_solution(6252755068329504193)
XLA Ops:
  0.0 1.7 %copy.12.rate_ref = f32[2,512,1]{2,1,0:T(8,128)} copy(f32[2,512,1]{1,0,2:T(2,128)} %bitcast.3) | data formatting | bytes 8192 | tf_op jit(solution)/shard_map/broadcast_in_dim;squeeze | solution.py:345
  1.7 2.0 %copy.11 = f32[1,512,256]{1,2,0:T(8,128)} copy(f32[1,512,256]{2,1,0:T(8,128)} %param.15) | data formatting | bytes 1048576 | tf_op args[6]
  3.7 123.9 %shard_map.91 = bf16[2,512,256]{2,1,0:T(8,128)(2,1)} custom-call(bf16[2,512,256]{2,1,0:T(8,128)(2,1)} %q_ref.1, bf16[2,512,256]{2,1,0:T(8,128)(2,1)} %k_ref.1, bf16[2,512,256]{2,1,0:T(8,128)(2,1)} %v_ref.1, f32[2,512,1]{2,1,0:T(8,128)} %copy.12.rate_ref, f32[1,256,512]{2,1,0:T(8,128)} %gate_ref.1, f32[1,256,512]{2,1,0:T(8,128)} %up_ref.1, ...), custom_call_target="tpu_custom_call" | custom-call | tf_op jit(solution)/shard_map/pallas_call | solution.py:317
  127.7 1.9 %copy.14 = bf16[2,512,256]{2,1,0:T(8,128)(2,1)} copy(bf16[2,512,256]{2,1,0:T(8,128)(2,1)} %shard_map.91) | data formatting | bytes 1048576

commit v2 on v1

--- a/solution.py
+++ b/solution.py
@@ -14,7 +14,7 @@
 
 NN = (((1,), (0,)), ((), ()))
 NT = (((1,), (1,)), ((), ()))
-COPIES = 120
+COPIES = 128
 
 
 def split(x):
@@ -27,7 +27,10 @@
 
 
 def dot3(a, b, dims=NN):
-    return dot1(a[0], b[0], dims) + (dot1(a[0], b[1], dims) + dot1(a[1], b[0], dims))
+    axis = dims[0][1][0]
+    left = jnp.concatenate([a[0], a[0], a[1]], axis=1)
+    right = jnp.concatenate([b[0], b[1], b[0]], axis=axis)
+    return dot1(left, right, dims)
 
 
 def unit_rows(x):
@@ -35,7 +38,7 @@
 
 
 def kernel(
-    q_ref, k_ref, v_ref, rate_ref, gate_ref, up_ref, downt_ref, gain_ref, proj_ref,
+    q_ref, k_ref, v_ref, rate_ref, gate_ref, up_ref, down_ref, gain_ref, proj_ref,
     out_ref,
     gate_now, up_now, down_now, sums, part, yslot, xown, xslot, full, halo, attended, projg, gath, iterate,
     send_sem, recv_sem, local_sem,
@@ -64,6 +67,9 @@
         started.append(copy)
         return copy
 
+    y_up = {"ctx": lax.rem(yi + 1, 4) * 2 + xh}
+    y_down = {"ctx": lax.rem(yi + 3, 4) * 2 + xh}
+
     def rows64(index):
         return pl.ds(pl.multiple_of(index * 64, 64), 64)
 
@@ -76,7 +82,7 @@
 
     gate_now[...] = gate_ref[0]
     up_now[...] = up_ref[0]
-    down_now[...] = downt_ref[0]
+    down_now[...] = down_ref[0].T
 
     def reduce_start(group, which, value):
         part[group, which] = value.astype(bf16)
@@ -98,12 +104,13 @@
         key_t = split(key_unit.T)
         gate_pre = dot3(key_two, split(gate_now[...]))
         up_pre = dot3(key_two, split(up_now[...]))
-        target = rate_ref[group] * v_ref[group].astype(f32)
+        if ready is not None:
+            ready()
+        rate_rows = jnp.broadcast_to(rate_ref[0, group : group + 1, :], (128, 512)).T[:, :1]
+        target = rate_rows * v_ref[group].astype(f32)
         sigma = jax.nn.sigmoid(gate_pre)
         gate_act = gate_pre * sigma
         grad_down = dot3(split(target.T), split(gate_act * up_pre))
-        if ready is not None:
-            ready()
         sends = {2: reduce_start(group, 2, grad_down)}
         back = dot3(split(target), split(down_now[...]))
         sends[1] = reduce_start(group, 1, dot3(key_t, split(back * gate_act)))
@@ -124,31 +131,56 @@
         copy.wait_recv()
         total = xown[group, which].astype(f32) + xslot[group, which].astype(f32)
         full[group, which, rows64(yi)] = total.astype(bf16)
-        return [
-            send(
-                full.at[group, which, rows64(yi)],
-                full.at[group, which, rows64(yi)],
-                {"ctx": lax.rem(yi + d, 4) * 2 + xh},
-            )
-            for d in (2, 1, 3)
-        ]
-
-    def orthogonal(group, which, now):
-        grads = full[group, which].astype(f32)
-        norm = jnp.sqrt(jnp.sum(grads * grads, keepdims=True)) + 1e-06
-        iterate[...] = grads / norm
-
+        ref = full.at[group, which, rows64(yi)]
+        return [send(ref, ref, y_up), send(ref, ref, y_down)]
+
+    def reduce_fourth(group, which, copies):
+        relays = []
+        for copy, source, half, where in ((copies[0], yi + 3, 0, y_up), (copies[1], yi + 1, 32, y_down)):
+            copy.wait_recv()
+            start = pl.multiple_of(lax.rem(source, 4) * 64 + half, 32)
+            ref = full.at[group, which, pl.ds(start, 32)]
+            relays.append(send(ref, ref, where))
+        return relays
+
+    def ortho_start(group, places):
+        for at in places:
+            grads = full[group, at].astype(f32)
+            norm = jnp.sqrt(jnp.sum(grads * grads, keepdims=True)) + 1e-06
+            iterate[at] = grads / norm
+
+    def ortho_sweeps(places, count):
         def sweep(_, carry):
-            x = iterate[...]
-            x2 = split(x)
-            gram = dot3(x2, x2, NT)
-            g2 = split(gram)
-            poly = -4.775 * gram + 2.0315 * dot3(g2, g2)
-            iterate[...] = 3.4445 * x + dot3(split(poly), x2)
+            x2 = {at: split(iterate[at]) for at in places}
+            gram = {at: dot3(x2[at], x2[at], NT) for at in places}
+            g2 = {at: split(gram[at]) for at in places}
+            poly = {at: -4.775 * gram[at] + 2.0315 * dot3(g2[at], g2[at]) for at in places}
+            p2 = {at: split(poly[at]) for at in places}
+            for at in places:
+                iterate[at] = 3.4445 * iterate[at] + dot3(p2[at], x2[at])
             return carry
 
-        lax.fori_loop(0, NS_ITERS, sweep, 0)
-        now[...] = now[...] + 0.5 * iterate[...]
+        lax.fori_loop(0, count, sweep, 0)
+
+    def ortho_finish(places):
+        for at in places:
+            now = (gate_now, up_now, down_now)[at]
+            now[...] = now[...] + 0.5 * iterate[at]
+
+    def update(group, spread):
+        relays = {2: reduce_fourth(group, 2, spread[2])}
+        for copy in relays[2]:
+            copy.wait_recv()
+        relays[1] = reduce_fourth(group, 1, spread[1])
+        relays[0] = reduce_fourth(group, 0, spread[0])
+        for which in (1, 0):
+            for copy in relays[which]:
+                copy.wait_recv()
+        yield
+        ortho_start(group, (2, 1, 0))
+        ortho_sweeps((2, 1, 0), NS_ITERS)
+        ortho_finish((2, 1, 0))
+        yield
 
     def attend(group):
         if group == 0:
@@ -177,13 +209,14 @@
             probs = (weights / jnp.sum(weights, axis=-1, keepdims=True)).astype(bf16)
             attended[group, block * 256 : block * 256 + 256] = dot1(probs, vals)
 
-    def apply_fast(group):
-        query = split(unit_rows(q_ref[group].astype(f32)))
+    def apply_fast(group, half):
+        rows = pl.ds(half * 256, 256)
+        query = split(unit_rows(q_ref[group, rows].astype(f32)))
         gate_pre = dot3(query, split(gate_now[...]))
         hidden = gate_pre * jax.nn.sigmoid(gate_pre) * dot3(query, split(up_now[...]))
         fast = dot3(split(hidden), split(down_now[...]), NT)
         normed = fast * lax.rsqrt(jnp.mean(fast * fast, axis=-1, keepdims=True) + 1e-05) * gain_ref[...]
-        gath[group, head] = (attended[group] + normed).astype(bf16)
+        gath[group, head, rows] = (attended[group, rows] + normed).astype(bf16)
 
     def name(xl_at, z_at, core_at):
         return xl_at * 8 + lax.rem(z_at + 4, 4) * 2 + core_at
@@ -197,71 +230,83 @@
         ref = gath.at[group, owner] if rows is None else gath.at[group, owner, rows]
         return send(ref, ref, where)
 
-    def gather_one(group):
-        return {
-            "sib": block_send(group, head, sibling),
-            "x": block_send(group, head, across),
-            "zp": block_send(group, head, above),
-            "zm": block_send(group, head, below),
-        }
-
-    def gather_two(group, c):
-        c["zp"].wait_recv()
-        c["f1"] = block_send(group, name(xl, z - 1, core), above, pl.ds(0, 256))
+    def half_rows(half):
+        return pl.ds(half * 256, 256)
+
+    def gather_z(group, half, c):
+        c["zp", half] = block_send(group, head, above, half_rows(half))
+        c["zm", half] = block_send(group, head, below, half_rows(half))
+
+    def gather_x(group, half, c):
+        c["x", half] = block_send(group, head, across, half_rows(half))
+
+    def gather_sibling(group, c):
+        c["sib"] = block_send(group, head, sibling)
+
+    def relay_x(group, half, c):
+        c["x", half].wait_recv()
+        c["xp", half] = block_send(group, name(1 - xl, z, core), above, half_rows(half))
+        c["xm", half] = block_send(group, name(1 - xl, z, core), below, half_rows(half))
+
+    def relay_z(group, half, c):
+        if half == 0:
+            c["zp", 0].wait_recv()
+            c["f", 0] = block_send(group, name(xl, z - 1, core), above, half_rows(0))
+        else:
+            c["zm", 1].wait_recv()
+            c["f", 1] = block_send(group, name(xl, z + 1, core), below, half_rows(1))
+
+    def relay_far(group, half, c):
+        c["f", half].wait_recv()
+        c["x2", half] = block_send(group, name(xl, z + 2, core), across, half_rows(half))
+
+    def share_near(group, c):
+        c["zp", 1].wait_recv()
         c["s1"] = block_send(group, name(xl, z - 1, core), sibling)
-        c["zm"].wait_recv()
-        c["f2"] = block_send(group, name(xl, z + 1, core), below, pl.ds(256, 256))
+        c["zm", 0].wait_recv()
         c["s2"] = block_send(group, name(xl, z + 1, core), sibling)
-        c["x"].wait_recv()
-        c["xp"] = block_send(group, name(1 - xl, z, core), above)
-        c["xm"] = block_send(group, name(1 - xl, z, core), below)
+
+    def share_across(group, c):
         c["s3"] = block_send(group, name(1 - xl, z, core), sibling)
 
-    def gather_three(group, c):
-        c["f1"].wait_recv()
-        c["f2"].wait_recv()
-        c["x2"] = block_send(group, name(xl, z + 2, core), across)
+    def share_far(group, c):
         c["s4"] = block_send(group, name(xl, z + 2, core), sibling)
-        c["xp"].wait_recv()
+
+    def share_sides(group, c):
+        for half in range(2):
+            c["xp", half].wait_recv()
         c["s5"] = block_send(group, name(1 - xl, z - 1, core), sibling)
-        c["xm"].wait_recv()
+        for half in range(2):
+            c["xm", half].wait_recv()
         c["s6"] = block_send(group, name(1 - xl, z + 1, core), sibling)
 
-    def gather_four(group, c):
-        c["x2"].wait_recv()
+    def share_last(group, c):
+        for half in range(2):
+            c["x2", half].wait_recv()
         c["s7"] = block_send(group, name(1 - xl, z + 2, core), sibling)
 
-    def arrived(c):
-        for key in ("sib", "s1", "s2", "s3", "s4", "s5", "s6", "s7"):
-            c[key].wait_recv()
-
-    def project(group):
-        total = None
-        for at in range(16):
-            term = dot1(gath[group, at], projg[at])
+    own_order = (
+        (xl, z), (xl, z - 1), (xl, z + 1), (1 - xl, z), (xl, z + 2), (1 - xl, z - 1), (1 - xl, z + 1), (1 - xl, z + 2)
+    )
+    shared = ("sib", "s1", "s2", "s3", "s4", "s5", "s6", "s7")
+
+    def project(group, total, own, c):
+        for at in own:
+            owner = name(*own_order[at], core)
+            term = dot1(gath[group, owner], projg[owner])
             total = term if total is None else total + term
-        out_ref[group] = total.astype(bf16)
-
-    halos = []
-
-    def on_ready():
-        pl.semaphore_wait(barrier, 22)
-
-    def on_ready_one():
-        return
-
-    sends = fast_grads(0, on_ready)
-    halos.append(halo_send(0))
-    cross = {which: reduce_second(0, which, sends[which]) for which in (2, 1, 0)}
-    spread = {which: reduce_third(0, which, cross[which]) for which in (2, 1, 0)}
-    halos.append(halo_send(1))
+        for at in own:
+            c[shared[at]].wait_recv()
+            owner = name(*own_order[at], 1 - core)
+            total = total + dot1(gath[group, owner], projg[owner])
+        return total
+
     mine = pltpu.make_async_copy(
         proj_ref.at[:, pl.ds(pl.multiple_of(head * 256, 256), 256)], projg.at[head], local_sem
     )
-    mine.start()
     exchange = []
-    for d in range(1, 16):
-        there = lax.rem(head + d, 16)
+
+    def exchange_with(there):
         exchange.append(
             send(
                 proj_ref.at[:, pl.ds(pl.multiple_of(there * 256, 256), 256)],
@@ -269,43 +314,79 @@
                 {"head": there},
             )
         )
+
+    def exchange_across(which):
+        for d in which:
+            exchange_with((1 - xl) * 8 + lax.rem(head + d, 8))
+
+    def on_ready():
+        pl.semaphore_wait(barrier, 22)
+        mine.start()
+        for d in range(1, 8):
+            exchange_with(xl * 8 + lax.rem(head + d, 8))
+        exchange_across(range(3))
+
+    order = (2, 1, 0)
+    sends = fast_grads(0, on_ready)
+    cross = {which: reduce_second(0, which, sends[which]) for which in order}
+    spread = {which: reduce_third(0, which, cross[which]) for which in order}
+    steps = update(0, spread)
+    next(steps)
+    halos = [halo_send(0), halo_send(1)]
+    next(steps)
+    exchange_across(range(3, 8))
+
+    sends = fast_grads(1)
+    near, last = {}, {}
     for copy in halos[0]:
         copy.wait_recv()
     attend(0)
-    for which, now in ((2, down_now), (1, up_now), (0, gate_now)):
-        for copy in spread[which]:
-            copy.wait_recv()
-        orthogonal(0, which, now)
-
-    sends = fast_grads(1)
-    apply_fast(0)
-    near = gather_one(0)
-    cross = {which: reduce_second(1, which, sends[which]) for which in (2, 1, 0)}
+    for half in range(2):
+        apply_fast(0, half)
+        gather_z(0, half, near)
+    gather_sibling(0, near)
+    cross = {which: reduce_second(1, which, sends[which]) for which in order}
+    for half in range(2):
+        gather_x(0, half, near)
+    spread = {which: reduce_third(1, which, cross[which]) for which in order}
+    for half in range(2):
+        relay_z(0, half, near)
+    steps = update(1, spread)
+    next(steps)
+    share_near(0, near)
+    for half in range(2):
+        relay_x(0, half, near)
+        relay_far(0, half, near)
+    share_across(0, near)
+    share_far(0, near)
     for copy in halos[1]:
         copy.wait_recv()
-    spread = {which: reduce_third(1, which, cross[which]) for which in (2, 1, 0)}
     attend(1)
-    gather_two(0, near)
-    for which, now in ((2, down_now), (1, up_now), (0, gate_now)):
-        for copy in spread[which]:
-            copy.wait_recv()
-        orthogonal(1, which, now)
-        if which == 2:
-            gather_three(0, near)
-        if which == 1:
-            gather_four(0, near)
-    apply_fast(1)
-    last = gather_one(1)
+    next(steps)
+    share_sides(0, near)
+    share_last(0, near)
+    for half in range(2):
+        apply_fast(1, half)
+        gather_x(1, half, last)
+        gather_z(1, half, last)
+    gather_sibling(1, last)
     mine.wait()
     for copy in exchange:
         copy.wait_recv()
-    arrived(near)
-    project(0)
-    gather_two(1, last)
-    gather_three(1, last)
-    gather_four(1, last)
-    arrived(last)
-    project(1)
+    out_ref[0] = project(0, None, range(8), near).astype(bf16)
+    for half in range(2):
+        relay_x(1, half, last)
+        relay_z(1, half, last)
+    share_near(1, last)
+    share_across(1, last)
+    total = project(1, None, range(4), last)
+    for half in range(2):
+        relay_far(1, half, last)
+    share_far(1, last)
+    share_sides(1, last)
+    total = project(1, total, range(4, 7), last)
+    share_last(1, last)
+    out_ref[1] = project(1, total, range(7, 8), last).astype(bf16)
     for copy in started:
         copy.wait_send()
 
@@ -333,7 +414,7 @@
             pltpu.VMEM((2, rows, width), f32),
             pltpu.VMEM((16, width, width), bf16),
             pltpu.VMEM((2, 16, rows, width), bf16),
-            pltpu.VMEM((width, hidden), f32),
+            pltpu.VMEM((3, width, hidden), f32),
             pltpu.SemaphoreType.DMA((COPIES,)),
             pltpu.SemaphoreType.DMA((COPIES,)),
             pltpu.SemaphoreType.DMA,
@@ -342,7 +423,7 @@
             collective_id=0, has_side_effects=True, vmem_limit_bytes=62 * 1024 * 1024
         ),
     )(
-        queries, keys, values, rates[0][:, :, None], w_gate, w_up, jnp.swapaxes(w_down, 1, 2), gains, out_proj
+        queries, keys, values, rates, w_gate, w_up, w_down, gains, out_proj
     )
 
 

time: 131 us -> 113 us (0.86)
  Pallas kernels: 124 us -> 111 us
  local copies, waits for them, and re-layouts: 5.61 us -> 1.87 us
    pallas_call x1, Pallas kernels: 124 us -> 111 us  [body(): pl.pallas_call(kernel, out_shape=jax.ShapeDtypeStruct((groups, rows, widt...]
    unnamed x2 -> x1, local copies, waits for them, and re-layouts: 3.9 us -> 1.87 us
    another operation x1 -> x0, local copies, waits for them, and re-layouts: 1.71 us -> none  [body(): rates[0][:, :, None]]
where the time goes in v2:
time: 113 us; the launch traced here: 112 us
  Pallas kernels  111 us (98%)
  local copies, waits for them, and re-layouts  1.87 us (2%)
    pallas_call x1, Pallas kernels, body(): pl.pallas_call(kernel, out_shape=jax.ShapeDtypeStruct((groups, rows, widt...  111 us

profile of v2, /device:TPU:1, one launch (start us, length us, event | category | flops | bytes accessed | tf_op | source)
XLA Modules:
  0.0 112.4 jit_solution(2823523786952057077)
XLA Ops:
  0.0 110.5 %shard_map.91 = bf16[2,512,256]{2,1,0:T(8,128)(2,1)} custom-call(bf16[2,512,256]{2,1,0:T(8,128)(2,1)} %q_ref.1, bf16[2,512,256]{2,1,0:T(8,128)(2,1)} %k_ref.1, bf16[2,512,256]{2,1,0:T(8,128)(2,1)} %v_ref.1, f32[1,2,512]{2,1,0:T(2,128)} %rate_ref.1, f32[1,256,512]{2,1,0:T(8,128)} %gate_ref.1, f32[1,256,512]{2,1,0:T(8,128)} %up_ref.1, ...), custom_call_target="tpu_custom_call" | custom-call | tf_op jit(solution)/shard_map/pallas_call | solution.py:398
  110.5 1.9 %copy.11 = bf16[2,512,256]{2,1,0:T(8,128)(2,1)} copy(bf16[2,512,256]{2,1,0:T(8,128)(2,1)} %shard_map.91) | data formatting | bytes 1048576

commit v3 on v2

--- a/solution.py
+++ b/solution.py
@@ -33,6 +33,10 @@
     return dot1(left, right, dims)
 
 
+def mirrored(whole, side):
+    return whole + (side + side.T)
+
+
 def unit_rows(x):
     return x / jnp.sqrt(jnp.sum(x * x, axis=-1, keepdims=True) + 1e-06)
 
@@ -40,7 +44,7 @@
 def kernel(
     q_ref, k_ref, v_ref, rate_ref, gate_ref, up_ref, down_ref, gain_ref, proj_ref,
     out_ref,
-    gate_now, up_now, down_now, sums, part, yslot, xown, xslot, full, halo, attended, projg, gath, iterate,
+    gate_now, up_now, down_now, part, yslot, xown, xslot, full, halo, attended, projg, gath, iterate,
     send_sem, recv_sem, local_sem,
 ):
     ctx = lax.axis_index("ctx")
@@ -66,9 +70,6 @@
         copy.start()
         started.append(copy)
         return copy
-
-    y_up = {"ctx": lax.rem(yi + 1, 4) * 2 + xh}
-    y_down = {"ctx": lax.rem(yi + 3, 4) * 2 + xh}
 
     def rows64(index):
         return pl.ds(pl.multiple_of(index * 64, 64), 64)
@@ -132,16 +133,7 @@
         total = xown[group, which].astype(f32) + xslot[group, which].astype(f32)
         full[group, which, rows64(yi)] = total.astype(bf16)
         ref = full.at[group, which, rows64(yi)]
-        return [send(ref, ref, y_up), send(ref, ref, y_down)]
-
-    def reduce_fourth(group, which, copies):
-        relays = []
-        for copy, source, half, where in ((copies[0], yi + 3, 0, y_up), (copies[1], yi + 1, 32, y_down)):
-            copy.wait_recv()
-            start = pl.multiple_of(lax.rem(source, 4) * 64 + half, 32)
-            ref = full.at[group, which, pl.ds(start, 32)]
-            relays.append(send(ref, ref, where))
-        return relays
+        return [send(ref, ref, {"ctx": lax.rem(yi + d, 4) * 2 + xh}) for d in (2, 1, 3)]
 
     def ortho_start(group, places):
         for at in places:
@@ -152,9 +144,12 @@
     def ortho_sweeps(places, count):
         def sweep(_, carry):
             x2 = {at: split(iterate[at]) for at in places}
-            gram = {at: dot3(x2[at], x2[at], NT) for at in places}
+            gram = {at: mirrored(dot1(x2[at][0], x2[at][0], NT), dot1(x2[at][0], x2[at][1], NT)) for at in places}
             g2 = {at: split(gram[at]) for at in places}
-            poly = {at: -4.775 * gram[at] + 2.0315 * dot3(g2[at], g2[at]) for at in places}
+            poly = {
+                at: -4.775 * gram[at] + 2.0315 * mirrored(dot1(g2[at][0], g2[at][0]), dot1(g2[at][0], g2[at][1]))
+                for at in places
+            }
             p2 = {at: split(poly[at]) for at in places}
             for at in places:
                 iterate[at] = 3.4445 * iterate[at] + dot3(p2[at], x2[at])
@@ -168,13 +163,8 @@
             now[...] = now[...] + 0.5 * iterate[at]
 
     def update(group, spread):
-        relays = {2: reduce_fourth(group, 2, spread[2])}
-        for copy in relays[2]:
-            copy.wait_recv()
-        relays[1] = reduce_fourth(group, 1, spread[1])
-        relays[0] = reduce_fourth(group, 0, spread[0])
-        for which in (1, 0):
-            for copy in relays[which]:
+        for which in (2, 1, 0):
+            for copy in spread[which]:
                 copy.wait_recv()
         yield
         ortho_start(group, (2, 1, 0))
@@ -404,7 +394,6 @@
             pltpu.VMEM((width, hidden), f32),
             pltpu.VMEM((width, hidden), f32),
             pltpu.VMEM((width, hidden), f32),
-            pltpu.VMEM((8, 128), f32),
             pltpu.VMEM((2, 3, width, hidden), bf16),
             pltpu.VMEM((2, 3, 3, 64, hidden), bf16),
             pltpu.VMEM((2, 3, 64, hidden), bf16),

time: 113 us -> 107 us (0.947)
  Pallas kernels: 111 us -> 105 us
    pallas_call x1, Pallas kernels: 111 us -> 105 us  [body(): pl.pallas_call(kernel, out_shape=jax.ShapeDtypeStruct((groups, rows, widt...]
where the time goes in v3:
time: 107 us
  Pallas kernels  105 us (98%)
  local copies, waits for them, and re-layouts  1.87 us (2%)
    pallas_call x1, Pallas kernels, body(): pl.pallas_call(kernel, out_shape=jax.ShapeDtypeStruct((groups, rows, widt...  105 us

profile of v3, /device:TPU:1, one launch (start us, length us, event | category | flops | bytes accessed | tf_op | source)
XLA Modules:
  0.0 106.8 jit_solution(15356258021451195670)
XLA Ops:
  0.0 104.9 %shard_map.91 = bf16[2,512,256]{2,1,0:T(8,128)(2,1)} custom-call(bf16[2,512,256]{2,1,0:T(8,128)(2,1)} %q_ref.1, bf16[2,512,256]{2,1,0:T(8,128)(2,1)} %k_ref.1, bf16[2,512,256]{2,1,0:T(8,128)(2,1)} %v_ref.1, f32[1,2,512]{2,1,0:T(2,128)} %rate_ref.1, f32[1,256,512]{2,1,0:T(8,128)} %gate_ref.1, f32[1,256,512]{2,1,0:T(8,128)} %up_ref.1, ...), custom_call_target="tpu_custom_call" | custom-call | tf_op jit(solution)/shard_map/pallas_call | solution.py:388
  104.9 1.9 %copy.11 = bf16[2,512,256]{2,1,0:T(8,128)(2,1)} copy(bf16[2,512,256]{2,1,0:T(8,128)(2,1)} %shard_map.91) | data formatting | bytes 1048576

commit v4 on v3

--- a/solution.py
+++ b/solution.py
@@ -322,9 +322,9 @@
     spread = {which: reduce_third(0, which, cross[which]) for which in order}
     steps = update(0, spread)
     next(steps)
-    halos = [halo_send(0), halo_send(1)]
+    halos = [halo_send(0)]
+    exchange_across(range(3, 8))
     next(steps)
-    exchange_across(range(3, 8))
 
     sends = fast_grads(1)
     near, last = {}, {}
@@ -349,10 +349,11 @@
         relay_far(0, half, near)
     share_across(0, near)
     share_far(0, near)
+    halos.append(halo_send(1))
+    next(steps)
     for copy in halos[1]:
         copy.wait_recv()
     attend(1)
-    next(steps)
     share_sides(0, near)
     share_last(0, near)
     for half in range(2):

time: 107 us -> 104 us (0.972)
  Pallas kernels: 105 us -> 101 us
    pallas_call x1, Pallas kernels: 105 us -> 101 us  [body(): pl.pallas_call(kernel, out_shape=jax.ShapeDtypeStruct((groups, rows, widt...]
where the time goes in v4:
time: 104 us; the launch traced here: 103 us
  Pallas kernels  101 us (97%)
  local copies, waits for them, and re-layouts  1.87 us (2%)
    pallas_call x1, Pallas kernels, body(): pl.pallas_call(kernel, out_shape=jax.ShapeDtypeStruct((groups, rows, widt...  101 us

profile of v4, /device:TPU:1, one launch (start us, length us, event | category | flops | bytes accessed | tf_op | source)
XLA Modules:
  0.0 102.9 jit_solution(7364601440990610821)
XLA Ops:
  0.0 101.0 %shard_map.91 = bf16[2,512,256]{2,1,0:T(8,128)(2,1)} custom-call(bf16[2,512,256]{2,1,0:T(8,128)(2,1)} %q_ref.1, bf16[2,512,256]{2,1,0:T(8,128)(2,1)} %k_ref.1, bf16[2,512,256]{2,1,0:T(8,128)(2,1)} %v_ref.1, f32[1,2,512]{2,1,0:T(2,128)} %rate_ref.1, f32[1,256,512]{2,1,0:T(8,128)} %gate_ref.1, f32[1,256,512]{2,1,0:T(8,128)} %up_ref.1, ...), custom_call_target="tpu_custom_call" | custom-call | tf_op jit(solution)/shard_map/pallas_call | solution.py:389
  101.0 1.9 %copy.11 = bf16[2,512,256]{2,1,0:T(8,128)(2,1)} copy(bf16[2,512,256]{2,1,0:T(8,128)(2,1)} %shard_map.91) | data formatting | bytes 1048576

commit v5 on v4

--- a/solution.py
+++ b/solution.py
@@ -88,7 +88,7 @@
     def reduce_start(group, which, value):
         part[group, which] = value.astype(bf16)
         own = []
-        for d in (2, 1, 3):
+        for d in (1, 3, 2):
             there = lax.rem(yi + d, 4)
             own.append(
                 send(
@@ -133,7 +133,7 @@
         total = xown[group, which].astype(f32) + xslot[group, which].astype(f32)
         full[group, which, rows64(yi)] = total.astype(bf16)
         ref = full.at[group, which, rows64(yi)]
-        return [send(ref, ref, {"ctx": lax.rem(yi + d, 4) * 2 + xh}) for d in (2, 1, 3)]
+        return [send(ref, ref, {"ctx": lax.rem(yi + d, 4) * 2 + xh}) for d in (1, 3, 2)]
 
     def ortho_start(group, places):
         for at in places:

time: 104 us -> 102 us (0.981); the launches traced: 103 us -> 102 us
  no operation moved by 1% of the time
where the time goes in v5:
time: 102 us
  Pallas kernels  100 us (98%)
  local copies, waits for them, and re-layouts  1.87 us (2%)
    pallas_call x1, Pallas kernels, body(): pl.pallas_call(kernel, out_shape=jax.ShapeDtypeStruct((groups, rows, widt...  100 us

profile of v5, /device:TPU:1, one launch (start us, length us, event | category | flops | bytes accessed | tf_op | source)
XLA Modules:
  0.0 102.0 jit_solution(3744506179457756982)
XLA Ops:
  0.0 100.2 %shard_map.91 = bf16[2,512,256]{2,1,0:T(8,128)(2,1)} custom-call(bf16[2,512,256]{2,1,0:T(8,128)(2,1)} %q_ref.1, bf16[2,512,256]{2,1,0:T(8,128)(2,1)} %k_ref.1, bf16[2,512,256]{2,1,0:T(8,128)(2,1)} %v_ref.1, f32[1,2,512]{2,1,0:T(2,128)} %rate_ref.1, f32[1,256,512]{2,1,0:T(8,128)} %gate_ref.1, f32[1,256,512]{2,1,0:T(8,128)} %up_ref.1, ...), custom_call_target="tpu_custom_call" | custom-call | tf_op jit(solution)/shard_map/pallas_call | solution.py:389
  100.2 1.9 %copy.11 = bf16[2,512,256]{2,1,0:T(8,128)(2,1)} copy(bf16[2,512,256]{2,1,0:T(8,128)(2,1)} %shard_map.91) | data formatting | bytes 1048576
